TPU v7x, 32 devices: a whole 2x2x4 slice. The times are simulated.
32 devices in a mesh: exp: 8 (over y, x, core), tp: 4 (over z).
Axes of the slice: x: 2, y: 2, z: 4, core: 2. Of those that a mesh axis runs over, the one named last changes fastest.
Arguments:
- attn_part: bfloat16 [4, 256, 7168], P('tp', 'exp'), may hold values from -2.5 to 2.5
- resid: bfloat16 [256, 7168], P('exp', 'tp'), may hold values from -50 to 50
- refusal: float32 [7168], replicated, may hold values from -4 to 4
- norm_gain: float32 [7168], P('tp'), may hold values from 0.5 to 1.5
- route_ids: int32 [256, 8], P('exp'), may hold values from 0 to 31, all different within a row; in each aligned block of 32 rows (0 to 31, 32 to 63, ...) at most 16 rows name the same one
- gate_q: int32 [256, 8], P('exp'), may hold values from 16 to 255
- w_gate: bfloat16 [32, 7168, 2048], P('exp', None, 'tp'), may hold values from -0.0625 to 0.0625
- w_up: bfloat16 [32, 7168, 2048], P('exp', None, 'tp'), may hold values from -0.0625 to 0.0625
- w_down: bfloat16 [32, 2048, 7168], P('exp', 'tp'), may hold values from -0.125 to 0.125
Outputs:
- layer_out: bfloat16 [256, 7168], P('exp', 'tp')
Inputs may be any that keep to these rules, and one draw needn't show every extreme that they name: `route_ids`: each row names 8 different experts; in each aligned block of 32 rows (the tokens of one index of exp) no expert is named by more than 16 rows, a bound that some block reaches.
All inputs are finite; a program needn't handle non-finite values.
Results may differ from a plain program's by a relative error of at most 0.015.
Values may be sent and summed in bfloat16 or wider, within the bound.
No kernel may reach another device: no remote copies, remote signals or barrier semaphores. Data moves between devices by JAX's collectives and lax.ppermute only.
A program may use at most 256 MiB of HBM per device.

v0:
```python
import jax
import jax.numpy as jnp
from jax import lax
from jax.sharding import PartitionSpec as P

CAP = 16
EPSILON = 1e-06
GATE_UNIT = 128.0


def route_tables(route_ids, gate_q, experts, slot_count):
    row_count = route_ids.shape[0]
    matches = route_ids[:, :, None] == jnp.arange(experts, dtype=jnp.int32)[None, None, :]
    named_count = jnp.sum(matches.astype(jnp.int32), axis=1, dtype=jnp.int32)
    weight = jnp.sum(jnp.where(matches, gate_q[:, :, None], 0), axis=1, dtype=jnp.int32)
    before = jnp.cumsum(named_count, axis=0, dtype=jnp.int32) - named_count
    placed = (named_count[:, :, None] == 1) & (
        before[:, :, None] == jnp.arange(slot_count, dtype=jnp.int32)[None, None, :]
    )
    select = placed.reshape(row_count, experts * slot_count)
    scaled = jnp.where(placed, weight[:, :, None].astype(jnp.float32) / GATE_UNIT, 0.0)
    scaled = scaled.reshape(row_count, experts * slot_count)
    return (select.astype(jnp.bfloat16).T, scaled.astype(jnp.bfloat16))


def apply_experts(inputs, gate_weight, up_weight, down_weight):
    gate_act = jnp.einsum("sicd,idh->sich", inputs, gate_weight, preferred_element_type=jnp.float32)
    up_act = jnp.einsum("sicd,idh->sich", inputs, up_weight, preferred_element_type=jnp.float32)
    activation = (jax.nn.silu(gate_act) * up_act).astype(jnp.bfloat16)
    term = jnp.einsum("sich,ihd->sicd", activation, down_weight, preferred_element_type=jnp.float32)
    return term.astype(jnp.bfloat16)


def local(attn_part, resid, refusal, norm_gain, route_ids, gate_q, w_gate, w_up, w_down):
    highest = lax.Precision.HIGHEST
    tp_count = lax.axis_size("tp")
    exp_count = lax.axis_size("exp")
    full_width = refusal.shape[0]
    col_count = full_width // tp_count
    local_experts = w_gate.shape[0]
    experts = local_experts * exp_count
    attn_summed = lax.psum_scatter(
        attn_part[0].astype(jnp.float32).astype(jnp.bfloat16), "tp", scatter_dimension=1, tiled=True
    ).astype(jnp.float32)
    summed_heads = resid.astype(jnp.float32) + attn_summed
    unit = refusal * lax.rsqrt(jnp.sum(refusal * refusal) + EPSILON)
    unit_cols = lax.dynamic_slice_in_dim(unit, lax.axis_index("tp") * col_count, col_count, 0)
    along_part = jnp.dot(summed_heads, unit_cols, precision=highest)
    along, energy = lax.psum((along_part, jnp.sum(summed_heads * summed_heads, axis=1)), "tp")
    projected = summed_heads - along[:, None] * unit_cols[None, :]
    squares = energy - along * along * (2.0 - jnp.sum(unit * unit))
    inverse = lax.rsqrt(squares / full_width + EPSILON)
    normed = (projected * inverse[:, None] * norm_gain[None, :]).astype(jnp.bfloat16)
    select, scaled = route_tables(route_ids, gate_q, experts, CAP)
    full_rows = lax.all_gather(normed, "tp", axis=1, tiled=True)
    outgoing = jnp.dot(select, full_rows, preferred_element_type=jnp.float32).astype(jnp.bfloat16)
    outgoing = outgoing.reshape(exp_count, local_experts, CAP, full_width)
    expert_terms = apply_experts(
        lax.all_to_all(outgoing, "exp", split_axis=0, concat_axis=0, tiled=True),
        w_gate,
        w_up,
        w_down,
    )
    returned = lax.all_to_all(expert_terms, "exp", split_axis=0, concat_axis=0, tiled=True)
    partial_sum = jnp.dot(
        scaled, returned.reshape(experts * CAP, full_width), preferred_element_type=jnp.float32
    )
    mixed_cols = lax.psum_scatter(
        partial_sum.astype(jnp.bfloat16), "tp", scatter_dimension=1, tiled=True
    ).astype(jnp.float32)
    return (projected + mixed_cols).astype(jnp.bfloat16)


def solution(mesh):
    return jax.shard_map(
        local,
        mesh=mesh,
        in_specs=(
            P("tp", "exp", None),
            P("exp", "tp"),
            P(),
            P("tp"),
            P("exp", None),
            P("exp", None),
            P("exp", None, "tp"),
            P("exp", None, "tp"),
            P("exp", "tp", None),
        ),
        out_specs=P("exp", "tp"),
        check_vma=False,
    )
```

profile of v0, /device:TPU:0, one launch (start us, length us, event | category | flops | bytes accessed | tf_op | source)
XLA Modules:
  0.0 321.4 jit_solution(12197363555979041016)
XLA Ops:
  6.5 0.0 reduce-scatter.3.cloned.1.call-start
  6.5 0.7 reduce-scatter.3.cloned.1.call-update
  7.3 1.4 multiply_reduce_fusion.2
  9.3 1.4 multiply_reduce_fusion.1
  10.7 0.1 dynamic_slice.3
  10.8 0.8 copy.26
  11.5 0.8 copy.29
  12.3 0.2 convert_reduce_fusion
  12.4 0.1 reduce_window_sum.11
  12.5 0.1 copy.28
  12.6 0.1 copy.27
  12.7 0.1 eq.66
  13.4 0.1 fusion.35
  13.6 19.8 %reduce-scatter.3.cloned.1.call-done = bf16[32,1792]{1,0:T(8,128)(2,1)} async-done(((bf16[32,7168]{1,0:T(8,128)(2,1)}), bf16[32,1792]{1,0:T(8,128)(2,1)}) %reduce-scatter.3.cloned.1.call-update) | async-done | bytes 114704 | tf_op jit(solution)/shard_map/reduce_scatter | solution.py:42
  33.4 1.1 multiply_reduce_fusion
  34.5 1.2 convolution_bitcast_fusion
  35.7 8.7 %all-reduce = (f32[32]{0:T(128)S(1)}, f32[32]{0:T(128)S(1)}) all-reduce(f32[32]{0:T(128)S(1)} %multiply_reduce_fusion, f32[32]{0:T(128)S(1)} %convolution_bitcast_fusion), channel_id=1, replica_groups=mesh['exp'=8,'tp'=4] {'tp'}, use_global_device_ids=true, to_apply=%region_7.8 | all-reduce | flops 64 | bytes 512 | tf_op jit(solution)/shard_map/psum | solution.py:49
  44.4 1.1 multiply_convert_fusion
  45.5 14.5 %all_gather.3 = bf16[32,7168]{1,0:T(8,128)(2,1)S(1)} all-gather(bf16[32,1792]{1,0:T(8,128)(2,1)S(1)} %multiply_convert_fusion), channel_id=1, replica_groups=mesh['exp'=8,'tp'=4] {'tp'}, dimensions={1}, use_global_device_ids=true | all-gather | bytes 573440 | tf_op jit(solution)/shard_map/all_gather | solution.py:55
  59.9 2.0 convolution_convert_fusion
  62.0 86.6 %all_to_all.10 = bf16[8,4,16,7168]{3,2,1,0:T(8,128)(2,1)} all-to-all(bf16[8,4,16,7168]{3,2,1,0:T(8,128)(2,1)S(1)} %bitcast.55), channel_id=1, replica_groups=mesh['exp'=8,'tp'=4] {'exp'}, dimensions={0} | all-to-all | bytes 14680064 | tf_op jit(solution)/shard_map/all_to_all | solution.py:59
  148.6 13.5 %fusion.14 = f32[8,4,16,512]{3,2,0,1:T(8,128)S(1)} fusion(bf16[4,7168,512]{2,1,0:T(8,128)(2,1)} %param.15, bf16[8,4,16,7168]{3,2,1,0:T(8,128)(2,1)} %all_to_all.10), kind=kOutput, calls=%fused_computation.12 | convolution fusion | flops 3758096384 | bytes 37748736 | tf_op jit(solution)/shard_map/sicd,idh->sich/dot_general | solution.py:27
  162.1 15.5 %fusion.29 = bf16[8,4,16,512]{3,2,0,1:T(8,128)(2,1)S(1)} fusion(bf16[4,7168,512]{2,1,0:T(8,128)(2,1)} %param.16, bf16[8,4,16,7168]{3,2,1,0:T(8,128)(2,1)} %all_to_all.10, f32[8,4,16,512]{3,2,0,1:T(8,128)S(1)} %fusion.14), kind=kOutput, calls=%fused_computation.15 | convolution fusion | flops 3759669248 | bytes 38273024 | tf_op jit(solution)/shard_map/sicd,idh->sich/dot_general | solution.py:28
  177.6 16.3 %fusion.9 = bf16[8,4,16,7168]{3,2,0,1:T(8,128)(2,1)} fusion(bf16[8,4,16,512]{3,2,0,1:T(8,128)(2,1)S(1)} %fusion.29, bf16[4,512,7168]{2,1,0:T(8,128)(2,1)} %param.17), kind=kOutput, calls=%fused_computation.8 | convolution fusion | flops 3761766400 | bytes 37224448 | tf_op jit(solution)/shard_map/sich,ihd->sicd/dot_general | solution.py:30
  194.0 6.9 %copy.33 = bf16[8,4,16,7168]{3,2,1,0:T(8,128)(2,1)} copy(bf16[8,4,16,7168]{3,2,0,1:T(8,128)(2,1)} %fusion.9) | data formatting | bytes 14680064 | tf_op jit(solution)/shard_map/convert_element_type | solution.py:31
  200.8 4.8 %all-to-all-start.1 = ((bf16[8,4,16,7168]{3,2,1,0:T(8,128)(2,1)}), bf16[8,4,16,7168]{3,2,1,0:T(8,128)(2,1)}, u32[]{:S(2)}, u32[]{:S(2)}) async-start(bf16[8,4,16,7168]{3,2,1,0:T(8,128)(2,1)} %copy.33), calls=%async_computation.2 | async-start | bytes 14680064 | tf_op jit(solution)/shard_map/all_to_all | solution.py:64
  205.7 0.0 copy-start
  205.7 0.0 copy-start.1
  205.7 0.0 reduce-scatter.5.cloned.1.call-start
  205.8 0.1 copy.30
  205.8 0.1 select_convert_fusion
  205.9 82.6 %all-to-all-done.1 = bf16[8,4,16,7168]{3,2,1,0:T(8,128)(2,1)} async-done(((bf16[8,4,16,7168]{3,2,1,0:T(8,128)(2,1)}), bf16[8,4,16,7168]{3,2,1,0:T(8,128)(2,1)}, u32[]{:S(2)}, u32[]{:S(2)}) %all-to-all-start.1) | async-done | bytes 7340064 | tf_op jit(solution)/shard_map/all_to_all | solution.py:64
  288.5 5.3 %convolution_convert_fusion.1 = bf16[32,7168]{1,0:T(8,128)(2,1)} fusion(bf16[32,512]{0,1:T(8,128)(2,1)S(1)} %bitcast.56, bf16[512,7168]{1,0:T(8,128)(2,1)} %bitcast.15), kind=kOutput, calls=%fused_computation.9 | convolution fusion | flops 235110400 | bytes 7831552 | tf_op jit(solution)/shard_map/dot_general | solution.py:65
  293.8 0.0 reduce-scatter.5.cloned.1.call-update
  293.8 19.1 %reduce-scatter.5.cloned.1.call-done = bf16[32,1792]{1,0:T(8,128)(2,1)} async-done(((bf16[32,7168]{1,0:T(8,128)(2,1)}), bf16[32,1792]{1,0:T(8,128)(2,1)}) %reduce-scatter.5.cloned.1.call-update) | async-done | bytes 114704 | tf_op jit(solution)/shard_map/reduce_scatter | solution.py:68
  312.9 0.0 copy-done
  312.9 0.0 copy-done.1
  312.9 1.6 add_convert_fusion
  (6 shorter events, 0.0 us)
Async XLA Ops:
  6.5 26.8 %reduce-scatter.3.cloned.1.call-start = ((), (), s32[]{:S(2)}) async-start(), calls=%async_computation.4 | async-start | bytes 573440 | tf_op jit(solution)/shard_map/reduce_scatter | solution.py:42
  200.8 87.7 %all-to-all-start.1 = ((bf16[8,4,16,7168]{3,2,1,0:T(8,128)(2,1)}), bf16[8,4,16,7168]{3,2,1,0:T(8,128)(2,1)}, u32[]{:S(2)}, u32[]{:S(2)}) async-start(bf16[8,4,16,7168]{3,2,1,0:T(8,128)(2,1)} %copy.33), calls=%async_computation.2 | async-start | bytes 14680064 | tf_op jit(solution)/shard_map/all_to_all | solution.py:64
  205.7 107.3 %copy-start = (bf16[32,1792]{1,0:T(8,128)(2,1)S(1)}, bf16[32,1792]{1,0:T(8,128)(2,1)}, u32[]{:S(2)}) copy-start(bf16[32,1792]{1,0:T(8,128)(2,1)} %param.10) | copy-start | bytes 344068
  205.7 107.2 %copy-start.1 = (bf16[32,1792]{1,0:T(8,128)(2,1)S(1)}, bf16[32,1792]{1,0:T(8,128)(2,1)}, u32[]{:S(2)}) copy-start(bf16[32,1792]{1,0:T(8,128)(2,1)} %reduce-scatter.3.cloned.1.call-done) | copy-start | bytes 344068
  205.7 107.2 %reduce-scatter.5.cloned.1.call-start = ((), (), s32[]{:S(2)}) async-start(), calls=%async_computation.5 | async-start | bytes 573440 | tf_op jit(solution)/shard_map/reduce_scatter | solution.py:68
Sparse Core Ops, SparseCore 0:
  9.6 23.6 reduce-scatter.2
  293.9 18.9 reduce-scatter.4
where the time goes:
time: 322 us; the launch traced here: 321 us
  waiting for transfers between devices  122 us (38%)
  blocking collectives  110 us (34%)
  matrix products  53.8 us (17%)
  between operations  14.9 us (5%)
  local copies, waits for them, and re-layouts  8.82 us (3%)
  other arithmetic  6.99 us (2%)
  starting transfers between devices  4.89 us (2%)
    all_to_all x1, blocking collectives, local(): lax.all_to_all(outgoing, 'exp', split_axis=0, concat_axis=0, tiled=True)  86.6 us
    all_to_all x1, waiting for transfers between devices, local(): lax.all_to_all(expert_terms, 'exp', split_axis=0, concat_axis=0, tiled=True)  82.6 us
    reduce_scatter x1, waiting for transfers between devices, local(): lax.psum_scatter(attn_part[0].astype(jnp.float32).astype(jnp.bfloat16), '...  19.8 us
    reduce_scatter x1, waiting for transfers between devices, local(): lax.psum_scatter(partial_sum.astype(jnp.bfloat16), 'tp', scatter_dimensio...  19.1 us
    dot_general x1, matrix products, apply_experts(): jnp.einsum('sich,ihd->sicd', activation, down_weight, preferred_element_t...  16.3 us
    dot_general x1, matrix products, apply_experts(): jnp.einsum('sicd,idh->sich', inputs, up_weight, preferred_element_type=jn...  15.5 us
    all_gather x1, blocking collectives, local(): full_rows = lax.all_gather(normed, 'tp', axis=1, tiled=True)  14.5 us
    dot_general x1, matrix products, apply_experts(): jnp.einsum('sicd,idh->sich', inputs, gate_weight, preferred_element_type=...  13.5 us
  transfers between devices with their start and end apart: 3, of which 3 were waited for; matrix products, arithmetic and copies ran while one was open for 2% of the time, Pallas kernels for 0%

commit v1 on v0

--- a/solution.py
+++ b/solution.py
@@ -6,6 +6,18 @@
 CAP = 16
 EPSILON = 1e-06
 GATE_UNIT = 128.0
+
+
+def doubled_up(array, axis, dim):
+    ways, here, turn = (lax.axis_size(axis), lax.axis_index(axis), array.shape[dim])
+    line, have = (array, 1)
+    while have < ways:
+        line = jnp.concatenate(
+            [line, lax.ppermute(line, axis, [(d, (d - have) % ways) for d in range(ways)])],
+            axis=dim,
+        )
+        have = 2 * have
+    return jnp.roll(line, here * turn, axis=dim)
 
 
 def route_tables(route_ids, gate_q, experts, slot_count):
@@ -52,7 +64,7 @@
     inverse = lax.rsqrt(squares / full_width + EPSILON)
     normed = (projected * inverse[:, None] * norm_gain[None, :]).astype(jnp.bfloat16)
     select, scaled = route_tables(route_ids, gate_q, experts, CAP)
-    full_rows = lax.all_gather(normed, "tp", axis=1, tiled=True)
+    full_rows = doubled_up(normed, "tp", 1)
     outgoing = jnp.dot(select, full_rows, preferred_element_type=jnp.float32).astype(jnp.bfloat16)
     outgoing = outgoing.reshape(exp_count, local_experts, CAP, full_width)
     expert_terms = apply_experts(

time: 322 us -> 325 us (level)
  blocking collectives: 110 us -> 95.1 us
  waiting for transfers between devices: 122 us -> 133 us
  starting transfers between devices: 4.89 us -> 10.7 us
    all_gather x1 -> x0, blocking collectives: 14.5 us -> none  [local(): full_rows = lax.all_gather(normed, 'tp', axis=1, tiled=True)]
    ppermute x0 -> x2, waiting for transfers between devices: none -> 6.75 us  [doubled_up(): lax.ppermute(line, axis, [(d, (d - have) % ways) for d in range(ways)])]
    ppermute x0 -> x2, starting transfers between devices: none -> 5.85 us  [doubled_up(): lax.ppermute(line, axis, [(d, (d - have) % ways) for d in range(ways)])]
    reduce_scatter x1, waiting for transfers between devices: 19.1 us -> 22.8 us  [local(): lax.psum_scatter(partial_sum.astype(jnp.bfloat16), 'tp', scatter_dimensio...]
  transfers between devices with their start and end apart: 3 -> 5, of which waited for: 3 -> 5; matrix products, arithmetic and copies ran while one was open for 2% -> 2% of each run, Pallas kernels for 0% -> 0%
where the time goes in v1:
time: 325 us; the launch traced here: 324 us
  waiting for transfers between devices  133 us (41%)
  blocking collectives  95.1 us (29%)
  matrix products  53.9 us (17%)
  between operations  14.9 us (5%)
  starting transfers between devices  10.7 us (3%)
  local copies, waits for them, and re-layouts  8.88 us (3%)
  other arithmetic  7.03 us (2%)
    all_to_all x1, blocking collectives, local(): lax.all_to_all(outgoing, 'exp', split_axis=0, concat_axis=0, tiled=True)  86.4 us
    all_to_all x1, waiting for transfers between devices, local(): lax.all_to_all(expert_terms, 'exp', split_axis=0, concat_axis=0, tiled=True)  82.6 us
    reduce_scatter x1, waiting for transfers between devices, local(): lax.psum_scatter(partial_sum.astype(jnp.bfloat16), 'tp', scatter_dimensio...  22.8 us
    reduce_scatter x1, waiting for transfers between devices, local(): lax.psum_scatter(attn_part[0].astype(jnp.float32).astype(jnp.bfloat16), '...  20.4 us
    dot_general x1, matrix products, apply_experts(): jnp.einsum('sich,ihd->sicd', activation, down_weight, preferred_element_t...  16.3 us
    dot_general x1, matrix products, apply_experts(): jnp.einsum('sicd,idh->sich', inputs, up_weight, preferred_element_type=jn...  15.5 us
    dot_general x1, matrix products, apply_experts(): jnp.einsum('sicd,idh->sich', inputs, gate_weight, preferred_element_type=...  13.5 us
    psum x1, blocking collectives, local(): lax.psum((along_part, jnp.sum(summed_heads * summed_heads, axis=1)), 'tp')  8.7 us
  transfers between devices with their start and end apart: 5, of which 5 were waited for; matrix products, arithmetic and copies ran while one was open for 2% of the time, Pallas kernels for 0%

profile of v1, /device:TPU:0, one launch (start us, length us, event | category | flops | bytes accessed | tf_op | source)
XLA Modules:
  0.0 323.8 jit_solution(11772610131547825813)
XLA Ops:
  6.5 0.0 reduce-scatter.3.cloned.1.call-start
  6.5 0.7 reduce-scatter.3.cloned.1.call-update
  7.3 1.4 multiply_reduce_fusion.2
  9.3 1.4 multiply_reduce_fusion.1
  10.7 0.1 dynamic_slice.7
  10.8 0.8 copy.26
  11.5 0.8 copy.29
  12.9 20.4 %reduce-scatter.3.cloned.1.call-done = bf16[32,1792]{1,0:T(8,128)(2,1)} async-done(((bf16[32,7168]{1,0:T(8,128)(2,1)}), bf16[32,1792]{1,0:T(8,128)(2,1)}) %reduce-scatter.3.cloned.1.call-update) | async-done | bytes 114704 | tf_op jit(solution)/shard_map/reduce_scatter | solution.py:54
  33.4 1.1 multiply_reduce_fusion
  34.5 1.2 convolution_bitcast_fusion
  35.7 8.7 %all-reduce = (f32[32]{0:T(128)S(1)}, f32[32]{0:T(128)S(1)}) all-reduce(f32[32]{0:T(128)S(1)} %multiply_reduce_fusion, f32[32]{0:T(128)S(1)} %convolution_bitcast_fusion), channel_id=1, replica_groups=mesh['exp'=8,'tp'=4] {'tp'}, use_global_device_ids=true, to_apply=%region_7.8 | all-reduce | flops 64 | bytes 512 | tf_op jit(solution)/shard_map/psum | solution.py:61
  44.4 1.1 constant_dynamic-update-slice_fusion.5
  45.5 1.8 collective-permute-start
  47.3 0.2 convert_reduce_fusion
  47.4 3.2 %collective-permute-done = bf16[32,1792]{1,0:T(8,128)(2,1)S(1)} collective-permute-done((bf16[32,1792]{1,0:T(8,128)(2,1)S(1)}, bf16[32,1792]{1,0:T(8,128)(2,1)S(1)}, u32[]{:S(2)}, u32[]{:S(2)}) %collective-permute-start) | collective-permute-done | bytes 114720 | tf_op jit(solution)/shard_map/ppermute | solution.py:16
  50.7 4.1 %collective-permute-start.1 = (bf16[32,3584]{1,0:T(8,128)(2,1)S(1)}, bf16[32,3584]{1,0:T(8,128)(2,1)S(1)}, u32[]{:S(2)}, u32[]{:S(2)}) collective-permute-start(bf16[32,3584]{1,0:T(8,128)(2,1)S(1)} %pad_maximum_fusion), channel_id=1, source_target_pairs={{0,2},{1,3},{2,0},{3,1},{4,6},{5,7},{6,4},{7,5},{8,10},{9,11},{10,... | collective-permute-start | bytes 688136 | tf_op jit(solution)/shard_map/ppermute | solution.py:16
  54.8 0.1 reduce_window_sum.11
  54.8 0.1 copy.28
  54.9 0.1 copy.27
  55.0 0.1 eq.69
  55.1 0.1 fusion.36
  55.2 3.5 %collective-permute-done.1 = bf16[32,3584]{1,0:T(8,128)(2,1)S(1)} collective-permute-done((bf16[32,3584]{1,0:T(8,128)(2,1)S(1)}, bf16[32,3584]{1,0:T(8,128)(2,1)S(1)}, u32[]{:S(2)}, u32[]{:S(2)}) %collective-permute-start.1) | collective-permute-done | bytes 229408 | tf_op jit(solution)/shard_map/ppermute | solution.py:16
  58.8 2.1 convolution_convert_fusion
  61.0 86.4 %all_to_all.10 = bf16[8,4,16,7168]{3,2,1,0:T(8,128)(2,1)} all-to-all(bf16[8,4,16,7168]{3,2,1,0:T(8,128)(2,1)S(1)} %bitcast.54), channel_id=1, replica_groups=mesh['exp'=8,'tp'=4] {'exp'}, dimensions={0} | all-to-all | bytes 14680064 | tf_op jit(solution)/shard_map/all_to_all | solution.py:71
  147.4 13.5 %fusion.14 = f32[8,4,16,512]{3,2,0,1:T(8,128)S(1)} fusion(bf16[4,7168,512]{2,1,0:T(8,128)(2,1)} %param.15, bf16[8,4,16,7168]{3,2,1,0:T(8,128)(2,1)} %all_to_all.10), kind=kOutput, calls=%fused_computation.12 | convolution fusion | flops 3758096384 | bytes 37748736 | tf_op jit(solution)/shard_map/sicd,idh->sich/dot_general | solution.py:39
  160.9 15.5 %fusion.29 = bf16[8,4,16,512]{3,2,0,1:T(8,128)(2,1)S(1)} fusion(bf16[4,7168,512]{2,1,0:T(8,128)(2,1)} %param.16, bf16[8,4,16,7168]{3,2,1,0:T(8,128)(2,1)} %all_to_all.10, f32[8,4,16,512]{3,2,0,1:T(8,128)S(1)} %fusion.14), kind=kOutput, calls=%fused_computation.15 | convolution fusion | flops 3759669248 | bytes 38273024 | tf_op jit(solution)/shard_map/sicd,idh->sich/dot_general | solution.py:40
  176.4 16.3 %fusion.9 = bf16[8,4,16,7168]{3,2,0,1:T(8,128)(2,1)} fusion(bf16[8,4,16,512]{3,2,0,1:T(8,128)(2,1)S(1)} %fusion.29, bf16[4,512,7168]{2,1,0:T(8,128)(2,1)} %param.17), kind=kOutput, calls=%fused_computation.8 | convolution fusion | flops 3761766400 | bytes 37224448 | tf_op jit(solution)/shard_map/sich,ihd->sicd/dot_general | solution.py:42
  192.7 6.9 %copy.33 = bf16[8,4,16,7168]{3,2,1,0:T(8,128)(2,1)} copy(bf16[8,4,16,7168]{3,2,0,1:T(8,128)(2,1)} %fusion.9) | data formatting | bytes 14680064 | tf_op jit(solution)/shard_map/convert_element_type | solution.py:43
  199.6 4.8 %all-to-all-start.1 = ((bf16[8,4,16,7168]{3,2,1,0:T(8,128)(2,1)}), bf16[8,4,16,7168]{3,2,1,0:T(8,128)(2,1)}, u32[]{:S(2)}, u32[]{:S(2)}) async-start(bf16[8,4,16,7168]{3,2,1,0:T(8,128)(2,1)} %copy.33), calls=%async_computation.2 | async-start | bytes 14680064 | tf_op jit(solution)/shard_map/all_to_all | solution.py:76
  204.5 0.0 copy-start
  204.5 0.0 copy-start.1
  204.5 0.0 reduce-scatter.5.cloned.1.call-start
  204.6 0.1 copy.30
  204.6 0.1 select_convert_fusion
  204.7 82.6 %all-to-all-done.1 = bf16[8,4,16,7168]{3,2,1,0:T(8,128)(2,1)} async-done(((bf16[8,4,16,7168]{3,2,1,0:T(8,128)(2,1)}), bf16[8,4,16,7168]{3,2,1,0:T(8,128)(2,1)}, u32[]{:S(2)}, u32[]{:S(2)}) %all-to-all-start.1) | async-done | bytes 7340064 | tf_op jit(solution)/shard_map/all_to_all | solution.py:76
  287.3 5.3 %convolution_convert_fusion.1 = bf16[32,7168]{1,0:T(8,128)(2,1)} fusion(bf16[32,512]{0,1:T(8,128)(2,1)S(1)} %bitcast.55, bf16[512,7168]{1,0:T(8,128)(2,1)} %bitcast.15), kind=kOutput, calls=%fused_computation.9 | convolution fusion | flops 235110400 | bytes 7831552 | tf_op jit(solution)/shard_map/dot_general | solution.py:77
  292.5 0.0 reduce-scatter.5.cloned.1.call-update
  292.6 22.8 %reduce-scatter.5.cloned.1.call-done = bf16[32,1792]{1,0:T(8,128)(2,1)} async-done(((bf16[32,7168]{1,0:T(8,128)(2,1)}), bf16[32,1792]{1,0:T(8,128)(2,1)}) %reduce-scatter.5.cloned.1.call-update) | async-done | bytes 114704 | tf_op jit(solution)/shard_map/reduce_scatter | solution.py:80
  315.4 0.0 copy-done
  315.4 0.0 copy-done.1
  315.4 1.6 add_convert_fusion
  (12 shorter events, 0.1 us)
Async XLA Ops:
  6.5 26.8 %reduce-scatter.3.cloned.1.call-start = ((), (), s32[]{:S(2)}) async-start(), calls=%async_computation.4 | async-start | bytes 573440 | tf_op jit(solution)/shard_map/reduce_scatter | solution.py:54
  45.5 5.2 %collective-permute-start = (bf16[32,1792]{1,0:T(8,128)(2,1)S(1)}, bf16[32,1792]{1,0:T(8,128)(2,1)S(1)}, u32[]{:S(2)}, u32[]{:S(2)}) collective-permute-start(bf16[32,1792]{1,0:T(8,128)(2,1)S(1)} %get-tuple-element.10), channel_id=1, source_target_pairs={{0,3},{1,0},{2,1},{3,2},{4,7},{5,4},{6,5},{7,6},{8,11},{9,8},{10,9... | collective-permute-start | bytes 344072 | tf_op jit(solution)/shard_map/ppermute | solution.py:16
  50.7 8.1 %collective-permute-start.1 = (bf16[32,3584]{1,0:T(8,128)(2,1)S(1)}, bf16[32,3584]{1,0:T(8,128)(2,1)S(1)}, u32[]{:S(2)}, u32[]{:S(2)}) collective-permute-start(bf16[32,3584]{1,0:T(8,128)(2,1)S(1)} %pad_maximum_fusion), channel_id=1, source_target_pairs={{0,2},{1,3},{2,0},{3,1},{4,6},{5,7},{6,4},{7,5},{8,10},{9,11},{10,... | collective-permute-start | bytes 688136 | tf_op jit(solution)/shard_map/ppermute | solution.py:16
  199.6 87.7 %all-to-all-start.1 = ((bf16[8,4,16,7168]{3,2,1,0:T(8,128)(2,1)}), bf16[8,4,16,7168]{3,2,1,0:T(8,128)(2,1)}, u32[]{:S(2)}, u32[]{:S(2)}) async-start(bf16[8,4,16,7168]{3,2,1,0:T(8,128)(2,1)} %copy.33), calls=%async_computation.2 | async-start | bytes 14680064 | tf_op jit(solution)/shard_map/all_to_all | solution.py:76
  204.5 110.9 %copy-start = (bf16[32,1792]{1,0:T(8,128)(2,1)S(1)}, bf16[32,1792]{1,0:T(8,128)(2,1)}, u32[]{:S(2)}) copy-start(bf16[32,1792]{1,0:T(8,128)(2,1)} %param.10) | copy-start | bytes 344068
  204.5 110.9 %copy-start.1 = (bf16[32,1792]{1,0:T(8,128)(2,1)S(1)}, bf16[32,1792]{1,0:T(8,128)(2,1)}, u32[]{:S(2)}) copy-start(bf16[32,1792]{1,0:T(8,128)(2,1)} %reduce-scatter.3.cloned.1.call-done) | copy-start | bytes 344068
  204.5 110.9 %reduce-scatter.5.cloned.1.call-start = ((), (), s32[]{:S(2)}) async-start(), calls=%async_computation.5 | async-start | bytes 573440 | tf_op jit(solution)/shard_map/reduce_scatter | solution.py:80
Sparse Core Ops, SparseCore 0:
  9.6 23.6 reduce-scatter.2
  292.7 22.6 reduce-scatter.4
